TPU v7x, 512 devices: a whole 4x8x8 slice. The times are simulated.
512 devices in a mesh: group: 8 (over x, z_lo), shard: 64 (over z_hi, y, core).
Axes of the slice: x: 4, y: 8, z: 8 (z_hi: 4, z_lo: 2; z = z_hi * 2 + z_lo), core: 2. Of those that a mesh axis runs over, the one named last changes fastest.
Arguments:
- tokens: bfloat16 [512, 3072], P('group', 'shard'), may hold values from -6 to 6
- cotangent: bfloat16 [512, 3072], P('group', 'shard'), may hold values from -1.5 to 1.5
- expert_ids: int32 [512, 2], P('group'), may hold values from 0 to 7, all different within a row; in each aligned block of 64 rows (0 to 63, 64 to 127, ...) at most 36 rows name the same one
- route_weight: float32 [512, 2], P('group'), may hold values from 0.1 to 0.9
- w_gate: bfloat16 [8, 3072, 8192], P('group', None, 'shard'), may hold values from -0.109375 to 0.109375
- w_up: bfloat16 [8, 3072, 8192], P('group', None, 'shard'), may hold values from -0.109375 to 0.109375
- w_down: bfloat16 [8, 8192, 3072], P('group', 'shard'), may hold values from -0.109375 to 0.109375
Outputs:
- grad_tokens: bfloat16 [512, 3072], P('group', 'shard')
- grad_gate: bfloat16 [8, 3072, 8192], P('group', None, 'shard')
- grad_up: bfloat16 [8, 3072, 8192], P('group', None, 'shard')
Inputs may be any that keep to these rules, and one draw needn't show every extreme that they name: `expert_ids`: each token names 2 different experts. Among the 64 tokens of one aligned block (the tokens of one index of group), no expert is named by more than 36 tokens.
All inputs are finite; a program needn't handle non-finite values.
Results may differ from a plain program's by a relative error of at most 0.0064.
Values may be sent and summed in bfloat16 or wider, within the bound.
A program may use at most 64 MiB of HBM per device.

v0:
```python
import jax
import jax.numpy as jnp
from jax import lax
from jax.sharding import PartitionSpec as P

EXPERTS = 8
CAP = 36


exact_mode = lax.Precision.HIGHEST


def slot_table(expert_ids, capacity):
    experts_axis = jnp.arange(EXPERTS, dtype=jnp.int32)
    counted = jnp.sum(
        (expert_ids[:, :, None] == experts_axis[None, None, :]).astype(jnp.int32), axis=1
    )
    ranking = jnp.cumsum(counted, axis=0) - 1
    places = jnp.arange(capacity, dtype=jnp.int32)
    slot_map = (counted.T[:, None, :] == 1) & (ranking.T[:, None, :] == places[None, :, None])
    return (counted, slot_map)


def slot_scales(slot_map, expert_ids, route_weight):
    experts_axis = jnp.arange(EXPERTS, dtype=jnp.int32)
    per_expert = jnp.sum(
        jnp.where(
            expert_ids[:, :, None] == experts_axis[None, None, :],
            route_weight[:, :, None],
            jnp.float32(0.0),
        ),
        axis=1,
    )
    return jnp.einsum("ect,te->ec", slot_map.astype(jnp.float32), per_expert, precision=exact_mode)


def place_rows(slot_map, scales, inputs, cotangents):
    selector = slot_map.astype(jnp.bfloat16)
    picked_inputs = jnp.einsum(
        "ect,td->ecd", selector, inputs, preferred_element_type=jnp.float32
    ).astype(jnp.bfloat16)
    picked_cot = jnp.einsum("ect,td->ecd", selector, cotangents, preferred_element_type=jnp.float32)
    scaled_cot = (scales[:, :, None] * picked_cot).astype(jnp.bfloat16)
    return (picked_inputs, scaled_cot)


def slot_grads(slot_inputs, slot_cotangents, paired, down_weight):
    hidden_width = down_weight.shape[0]
    joined = jnp.dot(slot_inputs, paired, preferred_element_type=jnp.float32)
    gate_pre = joined[:, :hidden_width]
    up_value = joined[:, hidden_width:]
    sigmoid_gate = jax.nn.sigmoid(gate_pre)
    active = gate_pre * sigmoid_gate
    hidden_grad = lax.dot_general(
        slot_cotangents, down_weight, (((1,), (1,)), ((), ())), preferred_element_type=jnp.float32
    )
    gate_grad = (
        hidden_grad * up_value * sigmoid_gate * (1.0 + gate_pre * (1.0 - sigmoid_gate))
    ).astype(jnp.bfloat16)
    up_grad = (hidden_grad * active).astype(jnp.bfloat16)
    stacked = jnp.concatenate([gate_grad, up_grad], axis=1)
    input_grad = lax.dot_general(
        stacked, paired, (((1,), (1,)), ((), ())), preferred_element_type=jnp.float32
    )
    return (input_grad, stacked)


def source_partials(slot_inputs, stacked, sources):
    capacity = slot_inputs.shape[0] // sources

    def accumulate(source, running):
        begin = (source * capacity).astype(jnp.int32)
        piece_inputs = lax.dynamic_slice_in_dim(slot_inputs, begin, capacity, 0)
        piece_grads = lax.dynamic_slice_in_dim(stacked, begin, capacity, 0)
        partial_sum = lax.dot_general(
            piece_inputs, piece_grads, (((0,), (0,)), ((), ())), preferred_element_type=jnp.float32
        )
        return running + lax.optimization_barrier(partial_sum.astype(jnp.bfloat16)).astype(
            jnp.float32
        )

    initial = jnp.zeros((slot_inputs.shape[1], stacked.shape[1]), jnp.float32)
    return lax.fori_loop(jnp.int32(0), jnp.int32(sources), accumulate, initial)


def body(tokens, cotangent, expert_ids, route_weight, w_gate, w_up, w_down):
    groups = lax.axis_size("group")
    hidden_width = w_gate.shape[2]
    counted, slot_map = slot_table(expert_ids, CAP)
    scales = slot_scales(slot_map, expert_ids, route_weight)
    paired_local = jnp.concatenate([w_gate, w_up], axis=2)
    sent_inputs, sent_cot = place_rows(slot_map, scales, tokens, cotangent)
    part_inputs, part_cot = (
        lax.all_to_all(sent_inputs, "group", split_axis=0, concat_axis=1, tiled=True),
        lax.all_to_all(sent_cot, "group", split_axis=0, concat_axis=1, tiled=True),
    )
    slot_inputs, slot_cot = (
        lax.all_gather(part_inputs, "shard", axis=2, tiled=True),
        lax.all_gather(part_cot, "shard", axis=2, tiled=True),
    )
    input_grad, stacked = slot_grads(slot_inputs[0], slot_cot[0], paired_local[0], w_down[0])
    grads_rows = [input_grad]
    weight_totals = [source_partials(slot_inputs[0], stacked, groups)]
    slot_grad = jnp.stack(grads_rows)
    summed_rows = lax.psum_scatter(slot_grad, "shard", scatter_dimension=2, tiled=True)
    returned = lax.all_to_all(summed_rows, "group", split_axis=1, concat_axis=0, tiled=True)
    grad_total = jnp.einsum(
        "ect,ecd->td", slot_map.astype(jnp.float32), returned, precision=exact_mode
    )
    stacked_totals = jnp.stack(weight_totals)
    grad_gate = stacked_totals[:, :, :hidden_width].astype(jnp.bfloat16)
    grad_up = stacked_totals[:, :, hidden_width:].astype(jnp.bfloat16)
    return (grad_total.astype(jnp.bfloat16), grad_gate, grad_up)


def solution(mesh):
    in_specs = (
        P("group", "shard"),
        P("group", "shard"),
        P("group", None),
        P("group", None),
        P("group", None, "shard"),
        P("group", None, "shard"),
        P("group", "shard", None),
    )
    out_specs = (P("group", "shard"), P("group", None, "shard"), P("group", None, "shard"))
    return jax.shard_map(body, mesh=mesh, in_specs=in_specs, out_specs=out_specs, check_vma=False)
```

profile of v0, /device:TPU:1, one launch (start us, length us, event | category | flops | bytes accessed | tf_op | source)
XLA Modules:
  0.0 811.4 jit_solution(8384122965178680824)
XLA Ops:
  7.2 0.8 convert_reduce_fusion
  8.2 0.9 convolution_convert_fusion.1
  9.3 11.5 %all_to_all.36 = bf16[8,2,864]{2,1,0:T(2,128)(2,1)S(1)} all-to-all(bf16[8,2,864]{2,1,0:T(2,128)(2,1)S(1)} %reshape.42), channel_id=1, replica_groups=mesh['group'=8,'shard'=64] {'group'}, dimensions={0} | all-to-all | bytes 55296 | tf_op jit(solution)/shard_map/all_to_all | solution.py:94
  21.0 0.7 copy.46
  21.7 0.7 select_reduce_fusion
  22.5 0.2 fusion.13
  22.7 0.9 fusion.5
  23.7 7.5 all_to_all.37
  31.3 0.7 copy.45
  32.1 1.3 dynamic-slice
  34.1 76.7 %all-gather.5.cloned.1.call-done = bf16[1,288,3072]{1,2,0:T(8,128)(2,1)} async-done(((bf16[1,288,48]{1,2,0:T(8,128)(2,1)}), bf16[1,288,3072]{1,2,0:T(8,128)(2,1)}) %all-gather.5.cloned.1.call-update) | async-done | bytes 1769488 | tf_op jit(solution)/shard_map/all_gather | solution.py:98
  110.8 2.9 fusion.7
  113.7 82.8 %all-gather.3.cloned.1.call-done = bf16[1,288,3072]{1,2,0:T(8,128)(2,1)} async-done(((bf16[1,288,48]{1,2,0:T(8,128)(2,1)}), bf16[1,288,3072]{1,2,0:T(8,128)(2,1)}) %all-gather.3.cloned.1.call-update) | async-done | bytes 1769488 | tf_op jit(solution)/shard_map/all_gather | solution.py:99
  196.5 2.7 fusion.17
  199.2 2.4 convolution_bitcast_fusion
  201.6 2.4 copy.42
  204.0 10.6 %copy.38 = f32[1,288,3072]{1,0,2:T(1,128)} copy(f32[1,288,3072]{2,1,0:T(8,128)} %convolution_bitcast_fusion) | data formatting | bytes 7077888 | tf_op jit(solution)/shard_map/stack | solution.py:104
  214.7 41.6 %while.11 = (s32[]{:T(128)}, f32[3072,256]{1,0:T(8,128)}, bf16[288,3072]{1,0:T(8,128)(2,1)}, bf16[288,256]{1,0:T(8,128)(2,1)S(1)}, s32[]{:T(128)}, /*index=5*/s32[]{:T(128)}, s32[]{:T(128)}, s32[]{:T(128)}) while((s32[]{:T(128)}, f32[3072,256]{1,0:T(8,128)}, bf16[288,3072]{1,0:T(8,128)(2,1)}, bf16[288,256]{1,0:T(8,128)(2,1)S(1)}, ...), condition=%wide.region_5.6_spmd.clone, body=%wide.region_4.5_spmd.clone.sunk | while | flops 59768836 | bytes 9704589 | solution.py:83
  214.7 1.6 convolution_convert_fusion.3
  216.3 1.9 select_add_fusion.2
  218.2 1.6 convolution_convert_fusion.3
  219.8 3.8 select_add_fusion.2
  223.7 1.6 convolution_convert_fusion.3
  225.3 3.8 select_add_fusion.2
  229.1 1.6 convolution_convert_fusion.3
  230.7 3.8 select_add_fusion.2
  234.5 1.6 convolution_convert_fusion.3
  236.1 3.9 select_add_fusion.2
  240.0 1.6 convolution_convert_fusion.3
  241.6 3.8 select_add_fusion.2
  245.4 1.6 convolution_convert_fusion.3
  247.0 3.8 select_add_fusion.2
  250.8 1.6 convolution_convert_fusion.3
  252.4 3.9 select_add_fusion.2
  256.3 2.0 convert_bitcast_fusion
  258.3 530.2 %all-reduce.3.cloned.1.call-done = f32[1,288,3072]{1,0,2:T(1,128)} async-done(((f32[1,288,3072]{1,0,2:T(1,128)}), f32[1,288,3072]{1,0,2:T(1,128)}) %all-reduce.3.cloned.1.call-update) | async-done | bytes 3538960
  788.6 0.9 constant_dynamic-slice_fusion
  789.6 0.5 broadcast.32
  790.1 1.0 reduce.5
  791.1 0.8 reshape.44
  791.9 4.2 all-to-all-start.2
  796.1 1.2 fusion.31
  797.3 4.0 all-to-all-done.2
  801.3 0.8 reduce.6
  802.1 0.3 reshape.45
  802.4 0.5 broadcast.31
  802.9 1.0 bitcast_reduce_fusion
  804.0 0.9 fusion.6
  (29 shorter events, 1.2 us)
Async XLA Ops:
  7.2 189.3 %copy-start = (bf16[1,128,3072]{2,1,0:T(8,128)(2,1)S(1)}, bf16[1,128,3072]{2,1,0:T(8,128)(2,1)}, u32[]{:S(2)}) copy-start(bf16[1,128,3072]{2,1,0:T(8,128)(2,1)} %param.15) | copy-start | bytes 2359300
  7.2 103.6 %all-gather.5.cloned.1.call-start = ((), (), s32[]{:S(2)}) async-start(), calls=%async_computation.4 | async-start | bytes 2396160 | tf_op jit(solution)/shard_map/all_gather | solution.py:98
  21.7 174.8 %all-gather.3.cloned.1.call-start = ((), (), s32[]{:S(2)}) async-start(), calls=%async_computation.3 | async-start | bytes 2396160 | tf_op jit(solution)/shard_map/all_gather | solution.py:99
  32.1 756.5 %all-reduce.3.cloned.1.call-start = ((), (), s32[]{:S(2)}) async-start(), calls=%async_computation.5 | async-start | bytes 9437184
  196.5 2.7 copy-start.2
  196.5 2.7 copy-start.3
  199.2 2.4 copy-start.1
  791.9 9.4 %all-to-all-start.2 = ((f32[8,1,1728]{2,1,0:T(1,128)}), f32[8,1,1728]{2,1,0:T(1,128)S(1)}, u32[]{:S(2)}, u32[]{:S(2)}) async-start(f32[8,1,1728]{2,1,0:T(1,128)} %reshape.44), calls=%async_computation.2 | async-start | bytes 114688 | tf_op jit(solution)/shard_map/all_to_all | solution.py:106
Sparse Core Ops, SparseCore 0:
  21.8 88.8 all-gather.4
  114.5 81.9 all-gather.2
  214.8 573.7 all-reduce.2
where the time goes:
time: 813 us; the launch traced here: 811 us
  waiting for transfers between devices  694 us (85%)
  other arithmetic  34.2 us (4%)
  matrix products  23.6 us (3%)
  local copies, waits for them, and re-layouts  21.8 us (3%)
  blocking collectives  19 us (2%)
  between operations  14.6 us (2%)
    unnamed x4, waiting for transfers between devices  530 us
    all_gather x1, waiting for transfers between devices, body(): lax.all_gather(part_cot, 'shard', axis=2, tiled=True)  82.8 us
    all_gather x1, waiting for transfers between devices, body(): lax.all_gather(part_inputs, 'shard', axis=2, tiled=True)  76.7 us
    add x8, other arithmetic, accumulate(): running + lax.optimization_barrier(partial_sum.astype(jnp.bfloat16)).asty...  28.8 us
  transfers between devices with their start and end apart: 4, of which 4 were waited for; matrix products, arithmetic and copies ran while one was open for 6% of the time, Pallas kernels for 0%

commit v1 on v0

v1 whole, which is shorter than its diff:
```python
import functools

import jax
import jax.numpy as jnp
from jax import lax
from jax.experimental import pallas as pl
from jax.experimental.pallas import tpu as pltpu
from jax.sharding import PartitionSpec as P

CAP = 36
LANES = 128
TOK_LANES = 384
ALL_LANES = 640
BF, F32 = jnp.bfloat16, jnp.float32
MESH = pl.DeviceIdType.MESH


def nt(a, b):
    return lax.dot_general(a, b, (((1,), (1,)), ((), ())), preferred_element_type=F32)


def nn(a, b):
    return lax.dot_general(a, b, (((1,), (0,)), ((), ())), preferred_element_type=F32)


def iota(shape, dim):
    return lax.broadcasted_iota(jnp.int32, shape, dim)


def kernel(
    dims, tok, cot, ids, wts, wg_hbm, wu_hbm, wd_hbm, out, gg_hbm, gu_hbm,
    wg, wu, wd, wt, picks, sent, got, spread, gath, dx, pair, ring_in, ring_out,
    zsum_out, zsum_in, pull, back, home, gbuf, ubuf, lsem, gsend, grecv, zsend, zrecv,
    ysend, yrecv, csend, crecv, psend, precv, rsend, rrecv, wsend, wrecv, hsend, hrecv,
):
    NG, ZH, NY, feat, toks = dims
    rows = feat * 2 * NY
    g = lax.axis_index("group")
    s = lax.axis_index("shard")
    c = lax.rem(s, 2)
    y = lax.rem(lax.div(s, 2), NY)
    z = lax.div(s, 2 * NY)

    def shard_id(zz, yy, cc):
        return (zz * NY + yy) * 2 + cc

    def wrap(v, n):
        return lax.rem(v + 2 * n, n)

    other = shard_id(z, y, 1 - c)
    right = shard_id(z, wrap(y + 1, NY), c)
    left = shard_id(z, wrap(y - 1, NY), c)

    barrier = pltpu.get_barrier_semaphore()

    def greet(gg, ss):
        pl.semaphore_signal(barrier, inc=1, device_id={"group": gg, "shard": ss}, device_id_type=MESH)

    for k in range(1, NG):
        greet(wrap(g + k, NG), s)
    for k in range(1, ZH):
        greet(g, shard_id(wrap(z + k, ZH), y, c))
    greet(g, right)
    greet(g, left)
    greet(g, other)

    loads = [
        pltpu.make_async_copy(h.at[0], v, lsem.at[i])
        for i, (h, v) in enumerate(((wg_hbm, wg), (wu_hbm, wu), (wd_hbm, wd)))
    ]
    for copy in loads:
        copy.start()

    def send(src, dst, ssem, rsem, gg, ss):
        copy = pltpu.make_async_remote_copy(
            src_ref=src, dst_ref=dst, send_sem=ssem, recv_sem=rsem,
            device_id={"group": gg, "shard": ss}, device_id_type=MESH,
        )
        copy.start()
        pending.append(copy)

    def arrived(dst, ssem, rsem, gg, ss):
        pltpu.make_async_remote_copy(
            src_ref=dst, dst_ref=dst, send_sem=ssem, recv_sem=rsem,
            device_id={"group": gg, "shard": ss}, device_id_type=MESH,
        ).wait_recv()

    pending = []

    who = iota((16, toks), 0)
    first, second = ids[0:1, :] == who, ids[1:2, :] == who
    hit = jnp.where(first, 1, 0) + jnp.where(second, 1, 0)
    upto = jnp.where(iota((toks, toks), 0) <= iota((toks, toks), 1), 1.0, 0.0).astype(BF)
    rank = nn(hit.astype(F32).astype(BF), upto).astype(jnp.int32) - 1
    rank = jnp.where((hit == 1) & (rank < CAP), rank, -1000)
    scale = jnp.where(first, wts[0:1, :], 0.0) + jnp.where(second, wts[1:2, :], 0.0)
    slot = iota((LANES, toks), 0)
    tok_b = tok[...]
    cot_f = cot[...].astype(F32)
    for e in range(NG):
        pick = jnp.where(slot == rank[e : e + 1, :], 1.0, 0.0).astype(BF)
        pick_cot = jnp.where(slot == rank[e : e + 1, :] + CAP, 1.0, 0.0).astype(BF)
        scaled = (cot_f * scale[e : e + 1, :]).astype(BF)
        picks[e] = pick
        sent[e] = (nt(tok_b, pick) + nt(scaled, pick_cot)).astype(BF)

    pl.semaphore_wait(barrier, (NG - 1) + (ZH - 1) + 3)

    for k in range(1, NG):
        e = wrap(g + k, NG)
        send(sent.at[e], got.at[g], gsend.at[k], grecv.at[NG - k], e, s)

    lane = iota((LANES, 1), 0)
    for e in range(NG):
        j = lane + CAP * e
        jc = j - CAP
        to = jnp.where(lane < CAP, j, jnp.where(jc < 256, jc + TOK_LANES, jc + 32))
        to = jnp.where(lane < 2 * CAP, to, -1)
        spread[e] = jnp.where(iota((LANES, ALL_LANES), 1) == to, 1.0, 0.0).astype(BF)
    got[g] = sent[g]
    for k in range(1, NG):
        e = wrap(g - k, NG)
        arrived(got.at[e], gsend.at[k], grecv.at[k], e, s)
    block = nn(got[0], spread[0])
    for e in range(1, NG):
        block = block + nn(got[e], spread[e])
    mine = pl.multiple_of(s * feat, 16)
    gath[pl.ds(mine, feat), :] = block.astype(BF)

    def place(zz, yy, cc):
        return gath.at[pl.ds(pl.multiple_of(shard_id(zz, yy, cc) * feat, 16), feat), :]

    reach = [[NY // 2, NY - 1 - NY // 2] if k % 2 == 0 else [NY - 1 - NY // 2, NY // 2] for k in range(ZH)]

    def pass_on(k, direction, t):
        step = 1 if direction == 0 else -1
        if t < reach[k][direction]:
            at = place(wrap(z + k, ZH), wrap(y - step * t, NY), c)
            send(at, at, ysend.at[k, direction, t], yrecv.at[k, direction, t], g, right if direction == 0 else left)

    def across(k, j):
        at = place(wrap(z + k, ZH), wrap(y + j, NY), c)
        send(at, at, csend.at[k, j], crecv.at[k, j], g, other)

    pass_on(0, 0, 0)
    pass_on(0, 1, 0)
    at = place(z, y, c)
    for k in range(1, ZH):
        to = shard_id(wrap(z + k, ZH), y, c)
        send(at, at, zsend.at[k], zrecv.at[ZH - k], g, to)
    across(0, 0)

    for copy in loads:
        copy.wait()
    eye = jnp.where(iota((LANES, LANES), 0) == iota((LANES, LANES), 1), 1.0, 0.0).astype(BF)
    depth = wg.shape[0]
    part = depth // 4
    for i in range(4):
        cols = slice(i * part, (i + 1) * part)
        wt[0:LANES, cols] = nt(eye, wg[cols, :]).astype(BF)
        wt[LANES : 2 * LANES, cols] = nt(eye, wu[cols, :]).astype(BF)

    order = [0] + [k for k in (1, ZH - 1) if 0 < k < ZH] + [2]
    order = list(dict.fromkeys(k for k in order if k < ZH))
    lag = {k: 0 if k == 0 else 1 for k in order}
    far = max(max(r) for r in reach)
    for wave in range(1, far + 2):
        for k in order:
            t = wave - lag[k]
            if t == 0 and k > 0:
                src = shard_id(wrap(z + k, ZH), y, c)
                arrived(place(wrap(z + k, ZH), y, c), zsend.at[k], zrecv.at[k], g, src)
                pass_on(k, 0, 0)
                pass_on(k, 1, 0)
                across(k, 0)
            for direction in (0, 1):
                step = 1 if direction == 0 else -1
                if 1 <= t <= reach[k][direction]:
                    at = place(wrap(z + k, ZH), wrap(y - step * t, NY), c)
                    arrived(at, ysend.at[k, direction, t - 1], yrecv.at[k, direction, t - 1], g, left if direction == 0 else right)
                    pass_on(k, direction, t)
                    across(k, (-step * t) % NY)
    for k in range(ZH):
        for j in range(NY):
            arrived(place(wrap(z + k, ZH), wrap(y + j, NY), 1 - c), csend.at[k, j], crecv.at[k, j], g, other)

    pre = nn(wt[...], gath[:, 0:TOK_LANES])
    hid = nn(wd[...], gath[:, 256:ALL_LANES])
    hid = jnp.concatenate([hid[:, 128:384], pltpu.roll(hid[:, 0:128], 96, 1)], axis=1)
    gate_pre, up_value = pre[0:LANES, :], pre[LANES : 2 * LANES, :]
    sig = 1.0 / (1.0 + jnp.exp(-gate_pre))
    live = iota((LANES, TOK_LANES), 1) < NG * CAP
    gate_grad = jnp.where(live, hid * up_value * sig * (1.0 + gate_pre * (1.0 - sig)), 0.0).astype(BF)
    up_grad = jnp.where(live, hid * gate_pre * sig, 0.0).astype(BF)

    many = 8 if NY % 8 == 0 else NY
    tall = many * feat
    pieces = (ZH * NY * 2) // many
    each = many // 2
    swaps = []
    for i in range(pieces):
        r = slice(i * tall, (i + 1) * tall)
        v = (nn(wg[r, :], gate_grad) + nn(wu[r, :], up_grad)).astype(BF)
        for m in range(each):
            for cc in range(2):
                dx[cc, i * each + m] = v[(2 * m + cc) * feat : (2 * m + cc + 1) * feat, :]
        here = pl.ds(i * each, each)
        send(dx.at[1 - c, here], pair.at[here], psend.at[i], precv.at[i], g, other)
    for i in range(pieces):
        here = pl.ds(i * each, each)
        arrived(pair.at[here], psend.at[i], precv.at[i], g, other)

    def own(k, yy):
        at = wrap(z + k, ZH) * NY + yy
        return dx[c, at].astype(F32) + pair[at].astype(F32)

    stores = []

    def weight_grads(i):
        r = slice(i * tall, (i + 1) * tall)
        x = gath[r, 0:TOK_LANES]
        gbuf[r, :] = nt(x, gate_grad).astype(BF)
        ubuf[r, :] = nt(x, up_grad).astype(BF)

    finish = [k for k in order if k][::-1] + [0]
    done = 0
    for t in range(1, far + 1):
        for k in finish:
            for direction in (0, 1):
                step = 1 if direction == 0 else -1
                length = reach[k][direction]
                if t > length:
                    continue
                v = own(k, wrap(y + step * (length - t + 1), NY))
                if t > 1:
                    at = ring_in.at[k, direction, t - 2]
                    arrived(at, rsend.at[k, direction, t - 2], rrecv.at[k, direction, t - 2], g, left if direction == 0 else right)
                    v = v + at[...].astype(F32)
                ring_out[k, direction, t - 1] = v.astype(BF)
                send(
                    ring_out.at[k, direction, t - 1], ring_in.at[k, direction, t - 1],
                    rsend.at[k, direction, t - 1], rrecv.at[k, direction, t - 1],
                    g, right if direction == 0 else left,
                )
        while done < min(pieces, t * -(-pieces // far)):
            weight_grads(done)
            done += 1
    for buf, hbm, n in ((gbuf, gg_hbm, 3), (ubuf, gu_hbm, 4)):
        copy = pltpu.make_async_copy(buf, hbm.at[0], lsem.at[n])
        copy.start()
        stores.append(copy)
    for e in range(NG):
        j = iota((TOK_LANES, LANES), 0) - CAP * e
        l = iota((TOK_LANES, LANES), 1)
        pull[e] = jnp.where((j == l) & (l < CAP), 1.0, 0.0).astype(BF)
    for k in finish:
        v = own(k, y)
        for direction in (0, 1):
            t = reach[k][direction]
            at = ring_in.at[k, direction, t - 1]
            arrived(at, rsend.at[k, direction, t - 1], rrecv.at[k, direction, t - 1], g, left if direction == 0 else right)
            v = v + at[...].astype(F32)
        if k:
            zsum_out[k] = v.astype(BF)
            to = shard_id(wrap(z + k, ZH), y, c)
            send(zsum_out.at[k], zsum_in.at[ZH - k], wsend.at[k], wrecv.at[ZH - k], g, to)
        else:
            total = v
    for k in range(1, ZH):
        src = shard_id(wrap(z + k, ZH), y, c)
        arrived(zsum_in.at[k], wsend.at[k], wrecv.at[k], g, src)
        total = total + zsum_in[k].astype(F32)
    total = total.astype(BF)

    for e in range(NG):
        back[e] = nn(total, pull[e]).astype(BF)
    for k in range(1, NG):
        e = wrap(g + k, NG)
        send(back.at[e], home.at[g], hsend.at[k], hrecv.at[NG - k], e, s)
    home[g] = back[g]
    for k in range(1, NG):
        e = wrap(g - k, NG)
        arrived(home.at[e], hsend.at[k], hrecv.at[k], e, s)
    res = nn(home[0], picks[0])
    for e in range(1, NG):
        res = res + nn(home[e], picks[e])
    out[...] = res.astype(BF)

    for copy in pending:
        copy.wait_send()
    for copy in stores:
        copy.wait()


def layout(shards):
    ny = 8 if shards == 64 else 4
    return shards // (2 * ny), ny


def body(tokens, cotangent, expert_ids, route_weight, w_gate, w_up, w_down):
    NG, NS = lax.axis_size("group"), lax.axis_size("shard")
    ZH, NY = layout(NS)
    toks, feat = tokens.shape
    depth = NS * feat
    far = NY // 2
    vmem = pl.BlockSpec(memory_space=pltpu.VMEM)
    hbm = pl.BlockSpec(memory_space=pl.ANY)
    dma = pltpu.SemaphoreType.DMA
    half = (ZH * NY, feat, TOK_LANES)
    ring = (ZH, 2, far, feat, TOK_LANES)
    pieces = (ZH * NY * 2) // (8 if NY % 8 == 0 else NY)
    out, gg, gu = pl.pallas_call(
        functools.partial(kernel, (NG, ZH, NY, feat, toks)),
        out_shape=(
            jax.ShapeDtypeStruct((feat, toks), BF),
            jax.ShapeDtypeStruct(w_gate.shape, BF),
            jax.ShapeDtypeStruct(w_up.shape, BF),
        ),
        in_specs=[vmem] * 4 + [hbm] * 3,
        out_specs=(vmem, hbm, hbm),
        scratch_shapes=[
            pltpu.VMEM((depth, LANES), BF),
            pltpu.VMEM((depth, LANES), BF),
            pltpu.VMEM((LANES, depth), BF),
            pltpu.VMEM((2 * LANES, depth), BF),
            pltpu.VMEM((NG, LANES, toks), BF),
            pltpu.VMEM((NG, feat, LANES), BF),
            pltpu.VMEM((NG, feat, LANES), BF),
            pltpu.VMEM((NG, LANES, ALL_LANES), BF),
            pltpu.VMEM((depth, ALL_LANES), BF),
            pltpu.VMEM((2,) + half, BF),
            pltpu.VMEM(half, BF),
            pltpu.VMEM(ring, BF),
            pltpu.VMEM(ring, BF),
            pltpu.VMEM((ZH, feat, TOK_LANES), BF),
            pltpu.VMEM((ZH, feat, TOK_LANES), BF),
            pltpu.VMEM((NG, TOK_LANES, LANES), BF),
            pltpu.VMEM((NG, feat, LANES), BF),
            pltpu.VMEM((NG, feat, LANES), BF),
            pltpu.VMEM((depth, LANES), BF),
            pltpu.VMEM((depth, LANES), BF),
            dma((5,)),
            dma((NG,)), dma((NG,)),
            dma((ZH,)), dma((ZH,)),
            dma((ZH, 2, far)), dma((ZH, 2, far)),
            dma((ZH, NY)), dma((ZH, NY)),
            dma((pieces,)), dma((pieces,)),
            dma((ZH, 2, far)), dma((ZH, 2, far)),
            dma((ZH,)), dma((ZH,)),
            dma((NG,)), dma((NG,)),
        ],
        compiler_params=pltpu.CompilerParams(collective_id=0, has_side_effects=True),
        name="moe_backward",
    )(tokens.T, cotangent.T, expert_ids.T, route_weight.T, w_gate, w_up, w_down)
    return out.T, gg, gu


def solution(mesh):
    in_specs = (
        P("group", "shard"),
        P("group", "shard"),
        P("group", None),
        P("group", None),
        P("group", None, "shard"),
        P("group", None, "shard"),
        P("group", "shard", None),
    )
    out_specs = (P("group", "shard"), P("group", None, "shard"), P("group", None, "shard"))
    return jax.shard_map(body, mesh=mesh, in_specs=in_specs, out_specs=out_specs, check_vma=False)
```

time: 813 us -> 82.7 us (0.10)
  the two profiles are of different devices: /device:TPU:1 before, /device:TPU:8 now
where the time goes in v1:
time: 82.7 us; the launch traced here: 82.4 us
  Pallas kernels  77.4 us (94%)
  local copies, waits for them, and re-layouts  4.33 us (5%)
    pallas_call x1, Pallas kernels, body(): pl.pallas_call(functools.partial(kernel, (NG, ZH, NY, feat, toks)), out_s...  77.4 us
    unnamed x5, local copies, waits for them, and re-layouts  4.33 us

profile of v1, /device:TPU:8, one launch (start us, length us, event | category | flops | bytes accessed | tf_op | source)
XLA Modules:
  0.0 82.4 jit_solution(2791910775070332637)
XLA Ops:
  0.6 77.4 %moe_backward.1 = (bf16[48,64]{1,0:T(8,128)(2,1)}, bf16[1,3072,128]{2,1,0:T(8,128)(2,1)}, bf16[1,3072,128]{2,1,0:T(8,128)(2,1)}) custom-call(bf16[48,64]{1,0:T(8,128)(2,1)} %bitcast.5, bf16[48,64]{1,0:T(8,128)(2,1)} %bitcast.6, s32[2,64]{1,0:T(2,128)} %bitcast.8, f32[2,64]{1,0:T(2,128)} %bitcast.9, bf16[1,3072,128]{2,1,0:T(8,128)(2,1)} %wg_hbm.1, ...), custom_call_target="tpu_custom_call" | custom-call | tf_op jit(solution)/shard_map/moe_backward/pallas_call | solution.py:312
  78.1 1.3 %copy.13 = bf16[64,48]{0,1:T(8,128)(2,1)} copy(bf16[64,48]{0,1:T(8,128)(2,1)} %bitcast.7) | data formatting | bytes 12288
  79.4 0.0 copy-start
  79.4 2.1 %copy.14 = bf16[1,3072,128]{2,1,0:T(8,128)(2,1)} copy(bf16[1,3072,128]{2,1,0:T(8,128)(2,1)} %get-tuple-element.13) | data formatting | bytes 1572864
  81.5 0.0 copy-done
  81.5 0.9 %copy.15 = bf16[1,3072,128]{2,1,0:T(8,128)(2,1)} copy(bf16[1,3072,128]{2,1,0:T(8,128)(2,1)S(1)} %copy-done) | data formatting | bytes 1572864
Async XLA Ops:
  79.4 2.1 %copy-start = (bf16[1,3072,128]{2,1,0:T(8,128)(2,1)S(1)}, bf16[1,3072,128]{2,1,0:T(8,128)(2,1)}, u32[]{:S(2)}) copy-start(bf16[1,3072,128]{2,1,0:T(8,128)(2,1)} %get-tuple-element.14) | copy-start | bytes 2359300

commit v2 on v1

--- a/solution.py
+++ b/solution.py
@@ -11,6 +11,8 @@
 LANES = 128
 TOK_LANES = 384
 ALL_LANES = 640
+HEAD = 256
+TAIL = 32
 BF, F32 = jnp.bfloat16, jnp.float32
 MESH = pl.DeviceIdType.MESH
 
@@ -29,7 +31,8 @@
 
 def kernel(
     dims, tok, cot, ids, wts, wg_hbm, wu_hbm, wd_hbm, out, gg_hbm, gu_hbm,
-    wg, wu, wd, wt, picks, sent, got, spread, gath, dx, pair, ring_in, ring_out,
+    wgu, wd, wt, picks, sent, got, spread, gath, dx, pair, dxt, pairt, ring_in, ring_out,
+    tail_in, tail_out,
     zsum_out, zsum_in, pull, back, home, gbuf, ubuf, lsem, gsend, grecv, zsend, zrecv,
     ysend, yrecv, csend, crecv, psend, precv, rsend, rrecv, wsend, wrecv, hsend, hrecv,
 ):
@@ -65,9 +68,11 @@
     greet(g, other)
 
     loads = [
-        pltpu.make_async_copy(h.at[0], v, lsem.at[i])
-        for i, (h, v) in enumerate(((wg_hbm, wg), (wu_hbm, wu), (wd_hbm, wd)))
+        pltpu.make_async_copy(wg_hbm.at[0], wgu.at[:, 0:LANES], lsem.at[0]),
+        pltpu.make_async_copy(wu_hbm.at[0], wgu.at[:, LANES : 2 * LANES], lsem.at[1]),
     ]
+    for q in range(ZH):
+        loads.append(pltpu.make_async_copy(wd_hbm.at[0, :, q * rows : (q + 1) * rows], wd.at[q], lsem.at[4 + q]))
     for copy in loads:
         copy.start()
 
@@ -118,6 +123,11 @@
         to = jnp.where(lane < 2 * CAP, to, -1)
         spread[e] = jnp.where(iota((LANES, ALL_LANES), 1) == to, 1.0, 0.0).astype(BF)
     got[g] = sent[g]
+    for copy in loads:
+        copy.wait()
+    eye = jnp.where(iota((2 * LANES, 2 * LANES), 0) == iota((2 * LANES, 2 * LANES), 1), 1.0, 0.0).astype(BF)
+    for q in range(ZH):
+        wt[q] = nt(eye, wgu[q * rows : (q + 1) * rows, :]).astype(BF)
     for k in range(1, NG):
         e = wrap(g - k, NG)
         arrived(got.at[e], gsend.at[k], grecv.at[k], e, s)
@@ -150,21 +160,22 @@
         send(at, at, zsend.at[k], zrecv.at[ZH - k], g, to)
     across(0, 0)
 
-    for copy in loads:
-        copy.wait()
-    eye = jnp.where(iota((LANES, LANES), 0) == iota((LANES, LANES), 1), 1.0, 0.0).astype(BF)
-    depth = wg.shape[0]
-    part = depth // 4
-    for i in range(4):
-        cols = slice(i * part, (i + 1) * part)
-        wt[0:LANES, cols] = nt(eye, wg[cols, :]).astype(BF)
-        wt[LANES : 2 * LANES, cols] = nt(eye, wu[cols, :]).astype(BF)
-
     order = [0] + [k for k in (1, ZH - 1) if 0 < k < ZH] + [2]
     order = list(dict.fromkeys(k for k in order if k < ZH))
     lag = {k: 0 if k == 0 else 1 for k in order}
     far = max(max(r) for r in reach)
+    def hidden(k, pre, hid):
+        for j in range(NY):
+            arrived(place(wrap(z + k, ZH), wrap(y + j, NY), 1 - c), csend.at[k, j], crecv.at[k, j], g, other)
+        q = wrap(z + k, ZH)
+        r = pl.ds(pl.multiple_of(q * rows, 16), rows)
+        return pre + nn(wt[q], gath[r, 0:TOK_LANES]), hid + nn(wd[q], gath[r, 256:ALL_LANES])
+
+    pre = jnp.zeros((2 * LANES, TOK_LANES), F32)
+    hid = jnp.zeros((LANES, TOK_LANES), F32)
     for wave in range(1, far + 2):
+        if wave == far + 1:
+            pre, hid = hidden(0, pre, hid)
         for k in order:
             t = wave - lag[k]
             if t == 0 and k > 0:
@@ -180,37 +191,45 @@
                     arrived(at, ysend.at[k, direction, t - 1], yrecv.at[k, direction, t - 1], g, left if direction == 0 else right)
                     pass_on(k, direction, t)
                     across(k, (-step * t) % NY)
-    for k in range(ZH):
-        for j in range(NY):
-            arrived(place(wrap(z + k, ZH), wrap(y + j, NY), 1 - c), csend.at[k, j], crecv.at[k, j], g, other)
-
-    pre = nn(wt[...], gath[:, 0:TOK_LANES])
-    hid = nn(wd[...], gath[:, 256:ALL_LANES])
+    for k in order[1:]:
+        pre, hid = hidden(k, pre, hid)
     hid = jnp.concatenate([hid[:, 128:384], pltpu.roll(hid[:, 0:128], 96, 1)], axis=1)
     gate_pre, up_value = pre[0:LANES, :], pre[LANES : 2 * LANES, :]
     sig = 1.0 / (1.0 + jnp.exp(-gate_pre))
     live = iota((LANES, TOK_LANES), 1) < NG * CAP
     gate_grad = jnp.where(live, hid * up_value * sig * (1.0 + gate_pre * (1.0 - sig)), 0.0).astype(BF)
     up_grad = jnp.where(live, hid * gate_pre * sig, 0.0).astype(BF)
-
-    many = 8 if NY % 8 == 0 else NY
-    tall = many * feat
-    pieces = (ZH * NY * 2) // many
-    each = many // 2
-    swaps = []
-    for i in range(pieces):
-        r = slice(i * tall, (i + 1) * tall)
-        v = (nn(wg[r, :], gate_grad) + nn(wu[r, :], up_grad)).astype(BF)
-        for m in range(each):
+    grads = jnp.concatenate([gate_grad, up_grad], axis=0)
+
+    def inputs(k):
+        q = wrap(z + k, ZH)
+        r = pl.ds(pl.multiple_of(q * rows, 16), rows)
+        v = nn(wgu[r, :], grads[:, 0:HEAD]).astype(BF)
+        for m in range(NY):
             for cc in range(2):
-                dx[cc, i * each + m] = v[(2 * m + cc) * feat : (2 * m + cc + 1) * feat, :]
-        here = pl.ds(i * each, each)
-        send(dx.at[1 - c, here], pair.at[here], psend.at[i], precv.at[i], g, other)
-    for i in range(pieces):
-        here = pl.ds(i * each, each)
-        arrived(pair.at[here], psend.at[i], precv.at[i], g, other)
+                dx[cc, q * NY + m] = v[(2 * m + cc) * feat : (2 * m + cc + 1) * feat, :]
+        here = pl.ds(q * NY, NY)
+        send(dx.at[1 - c, here], pair.at[here], psend.at[k], precv.at[k], g, other)
+
+    def tails():
+        last = grads[:, HEAD:TOK_LANES].astype(F32)
+        v = nn(wgu[0:rows, :], last.astype(BF))
+        for q in range(1, ZH):
+            v = v + nn(wgu[q * rows : (q + 1) * rows, :], pltpu.roll(last, TAIL * q, 1).astype(BF))
+        v = v.astype(BF)
+        for m in range(NY):
+            for cc in range(2):
+                dxt[cc, m] = v[(2 * m + cc) * feat : (2 * m + cc + 1) * feat, :]
+        send(dxt.at[1 - c], pairt, psend.at[ZH], precv.at[ZH], g, other)
+
+    def paired(k):
+        here = pl.ds(wrap(z + k, ZH) * NY, NY)
+        at = pairt if k == ZH else pair.at[here]
+        arrived(at, psend.at[k], precv.at[k], g, other)
 
     def own(k, yy):
+        if k == ZH:
+            return dxt[c, yy].astype(F32) + pairt[yy].astype(F32)
         at = wrap(z + k, ZH) * NY + yy
         return dx[c, at].astype(F32) + pair[at].astype(F32)
 
@@ -218,54 +237,78 @@
 
     def weight_grads(i):
         r = slice(i * tall, (i + 1) * tall)
-        x = gath[r, 0:TOK_LANES]
-        gbuf[r, :] = nt(x, gate_grad).astype(BF)
-        ubuf[r, :] = nt(x, up_grad).astype(BF)
+        v = nt(gath[r, 0:TOK_LANES], grads).astype(BF)
+        gbuf[r, :] = v[:, 0:LANES]
+        ubuf[r, :] = v[:, LANES : 2 * LANES]
 
     finish = [k for k in order if k][::-1] + [0]
+    finish = finish[:1] + [ZH] + finish[1:]
+    reach.append(reach[0])
+
+    def ring(k, t):
+        for direction in (0, 1):
+            step = 1 if direction == 0 else -1
+            length = reach[k][direction]
+            if t > length:
+                continue
+            v = own(k, wrap(y + step * (length - t + 1), NY))
+            into, outof = (tail_in, tail_out) if k == ZH else (ring_in.at[k], ring_out.at[k])
+            if t > 1:
+                at = into.at[direction, t - 2]
+                arrived(at, rsend.at[k, direction, t - 2], rrecv.at[k, direction, t - 2], g, left if direction == 0 else right)
+                v = v + at[...].astype(F32)
+            outof[direction, t - 1] = v.astype(BF)
+            send(
+                outof.at[direction, t - 1], into.at[direction, t - 1],
+                rsend.at[k, direction, t - 1], rrecv.at[k, direction, t - 1],
+                g, right if direction == 0 else left,
+            )
+
+    for i, k in enumerate(finish):
+        if k == ZH:
+            tails()
+        else:
+            inputs(k)
+        if i:
+            paired(finish[i - 1])
+            ring(finish[i - 1], 1)
+    paired(finish[-1])
+    ring(finish[-1], 1)
+    pieces = 2 * ZH
+    tall = rows // 2
     done = 0
-    for t in range(1, far + 1):
-        for k in finish:
-            for direction in (0, 1):
-                step = 1 if direction == 0 else -1
-                length = reach[k][direction]
-                if t > length:
-                    continue
-                v = own(k, wrap(y + step * (length - t + 1), NY))
-                if t > 1:
-                    at = ring_in.at[k, direction, t - 2]
-                    arrived(at, rsend.at[k, direction, t - 2], rrecv.at[k, direction, t - 2], g, left if direction == 0 else right)
-                    v = v + at[...].astype(F32)
-                ring_out[k, direction, t - 1] = v.astype(BF)
-                send(
-                    ring_out.at[k, direction, t - 1], ring_in.at[k, direction, t - 1],
-                    rsend.at[k, direction, t - 1], rrecv.at[k, direction, t - 1],
-                    g, right if direction == 0 else left,
-                )
-        while done < min(pieces, t * -(-pieces // far)):
+    for t in range(2, far + 1):
+        while done < min(pieces, (t - 1) * -(-pieces // (far - 1))):
             weight_grads(done)
             done += 1
+        for k in finish:
+            ring(k, t)
     for buf, hbm, n in ((gbuf, gg_hbm, 3), (ubuf, gu_hbm, 4)):
         copy = pltpu.make_async_copy(buf, hbm.at[0], lsem.at[n])
         copy.start()
         stores.append(copy)
     for e in range(NG):
-        j = iota((TOK_LANES, LANES), 0) - CAP * e
         l = iota((TOK_LANES, LANES), 1)
-        pull[e] = jnp.where((j == l) & (l < CAP), 1.0, 0.0).astype(BF)
-    for k in finish:
+        j = l + CAP * e
+        j = jnp.where(j < HEAD, j, j + TAIL * z)
+        pull[e] = jnp.where((iota((TOK_LANES, LANES), 0) == j) & (l < CAP), 1.0, 0.0).astype(BF)
+    for k in [ZH] + [k for k in finish if k < ZH]:
         v = own(k, y)
+        into = tail_in if k == ZH else ring_in.at[k]
         for direction in (0, 1):
             t = reach[k][direction]
-            at = ring_in.at[k, direction, t - 1]
+            at = into.at[direction, t - 1]
             arrived(at, rsend.at[k, direction, t - 1], rrecv.at[k, direction, t - 1], g, left if direction == 0 else right)
             v = v + at[...].astype(F32)
-        if k:
-            zsum_out[k] = v.astype(BF)
+        if k == ZH:
+            tail = v
+        elif k:
+            zsum_out[k, :, 0:HEAD] = v.astype(BF)
+            zsum_out[k, :, HEAD:TOK_LANES] = tail.astype(BF)
             to = shard_id(wrap(z + k, ZH), y, c)
             send(zsum_out.at[k], zsum_in.at[ZH - k], wsend.at[k], wrecv.at[ZH - k], g, to)
         else:
-            total = v
+            total = jnp.concatenate([v, tail], axis=1)
     for k in range(1, ZH):
         src = shard_id(wrap(z + k, ZH), y, c)
         arrived(zsum_in.at[k], wsend.at[k], wrecv.at[k], g, src)
@@ -292,6 +335,17 @@
         copy.wait()
 
 
+def finish(out_in, gg_in, gu_in, out, gg, gu, sem):
+    copies = [
+        pltpu.make_async_copy(a, b, sem.at[i])
+        for i, (a, b) in enumerate(((out_in, out), (gg_in, gg), (gu_in, gu)))
+    ]
+    for copy in copies:
+        copy.start()
+    for copy in copies:
+        copy.wait()
+
+
 def layout(shards):
     ny = 8 if shards == 64 else 4
     return shards // (2 * ny), ny
@@ -305,10 +359,11 @@
     far = NY // 2
     vmem = pl.BlockSpec(memory_space=pltpu.VMEM)
     hbm = pl.BlockSpec(memory_space=pl.ANY)
+    far_hbm = pl.BlockSpec(memory_space=pltpu.MemorySpace.HBM)
     dma = pltpu.SemaphoreType.DMA
-    half = (ZH * NY, feat, TOK_LANES)
-    ring = (ZH, 2, far, feat, TOK_LANES)
-    pieces = (ZH * NY * 2) // (8 if NY % 8 == 0 else NY)
+    half = (ZH * NY, feat, HEAD)
+    ring = (ZH, 2, far, feat, HEAD)
+    tail = (2, far, feat, LANES)
     out, gg, gu = pl.pallas_call(
         functools.partial(kernel, (NG, ZH, NY, feat, toks)),
         out_shape=(
@@ -316,13 +371,12 @@
             jax.ShapeDtypeStruct(w_gate.shape, BF),
             jax.ShapeDtypeStruct(w_up.shape, BF),
         ),
-        in_specs=[vmem] * 4 + [hbm] * 3,
+        in_specs=[vmem] * 4 + [far_hbm] * 3,
         out_specs=(vmem, hbm, hbm),
         scratch_shapes=[
-            pltpu.VMEM((depth, LANES), BF),
-            pltpu.VMEM((depth, LANES), BF),
-            pltpu.VMEM((LANES, depth), BF),
-            pltpu.VMEM((2 * LANES, depth), BF),
+            pltpu.VMEM((depth, 2 * LANES), BF),
+            pltpu.VMEM((ZH, LANES, depth // ZH), BF),
+            pltpu.VMEM((ZH, 2 * LANES, depth // ZH), BF),
             pltpu.VMEM((NG, LANES, toks), BF),
             pltpu.VMEM((NG, feat, LANES), BF),
             pltpu.VMEM((NG, feat, LANES), BF),
@@ -330,8 +384,12 @@
             pltpu.VMEM((depth, ALL_LANES), BF),
             pltpu.VMEM((2,) + half, BF),
             pltpu.VMEM(half, BF),
+            pltpu.VMEM((2, NY, feat, LANES), BF),
+            pltpu.VMEM((NY, feat, LANES), BF),
             pltpu.VMEM(ring, BF),
             pltpu.VMEM(ring, BF),
+            pltpu.VMEM(tail, BF),
+            pltpu.VMEM(tail, BF),
             pltpu.VMEM((ZH, feat, TOK_LANES), BF),
             pltpu.VMEM((ZH, feat, TOK_LANES), BF),
             pltpu.VMEM((NG, TOK_LANES, LANES), BF),
@@ -339,19 +397,31 @@
             pltpu.VMEM((NG, feat, LANES), BF),
             pltpu.VMEM((depth, LANES), BF),
             pltpu.VMEM((depth, LANES), BF),
-            dma((5,)),
+            dma((4 + ZH,)),
             dma((NG,)), dma((NG,)),
             dma((ZH,)), dma((ZH,)),
             dma((ZH, 2, far)), dma((ZH, 2, far)),
             dma((ZH, NY)), dma((ZH, NY)),
-            dma((pieces,)), dma((pieces,)),
-            dma((ZH, 2, far)), dma((ZH, 2, far)),
+            dma((ZH + 1,)), dma((ZH + 1,)),
+            dma((ZH + 1, 2, far)), dma((ZH + 1, 2, far)),
             dma((ZH,)), dma((ZH,)),
             dma((NG,)), dma((NG,)),
         ],
-        compiler_params=pltpu.CompilerParams(collective_id=0, has_side_effects=True),
+        compiler_params=pltpu.CompilerParams(collective_id=0, has_side_effects=True, vmem_limit_bytes=32 << 20),
         name="moe_backward",
-    )(tokens.T, cotangent.T, expert_ids.T, route_weight.T, w_gate, w_up, w_down)
+    )(*(
+        pltpu.with_memory_space_constraint(a, pltpu.MemorySpace.HBM)
+        for a in (tokens.T, cotangent.T, expert_ids.T, route_weight.T, w_gate, w_up, w_down)
+    ))
+    out, gg, gu = pl.pallas_call(
+        finish,
+        out_shape=tuple(jax.ShapeDtypeStruct(a.shape, a.dtype) for a in (out, gg, gu)),
+        in_specs=[hbm] * 3,
+        out_specs=(hbm,) * 3,
+        scratch_shapes=[dma((3,))],
+        compiler_params=pltpu.CompilerParams(vmem_limit_bytes=4 << 20),
+        name="finish",
+    )(out, gg, gu)
     return out.T, gg, gu
 
 

time: 82.7 us -> 76 us (0.919)
  the two profiles are of different devices: /device:TPU:8 before, /device:TPU:2 now
where the time goes in v2:
time: 76 us; the launch traced here: 75.8 us
  Pallas kernels  75.2 us (99%)
    pallas_call x1, Pallas kernels, body(): pl.pallas_call(functools.partial(kernel, (NG, ZH, NY, feat, toks)), out_s...  74 us

profile of v2, /device:TPU:2, one launch (start us, length us, event | category | flops | bytes accessed | tf_op | source)
XLA Modules:
  0.0 75.8 jit_solution(7351662510843945392)
XLA Ops:
  0.6 74.0 %moe_backward.1 = (bf16[48,64]{1,0:T(8,128)(2,1)S(1)}, bf16[1,3072,128]{2,1,0:T(8,128)(2,1)S(1)}, bf16[1,3072,128]{2,1,0:T(8,128)(2,1)S(1)}) custom-call(bf16[48,64]{1,0:T(8,128)(2,1)} %bitcast.5, bf16[48,64]{1,0:T(8,128)(2,1)} %bitcast.6, s32[2,64]{1,0:T(2,128)} %bitcast.7, f32[2,64]{1,0:T(2,128)} %bitcast.8, bf16[1,3072,128]{2,1,0:T(8,128)(2,1)} %wg_hbm.1, ...), custom_call_target="tpu_custom_call" | custom-call | tf_op jit(solution)/shard_map/moe_backward/pallas_call | solution.py:367
  74.6 1.2 %finish.1 = (bf16[48,64]{1,0:T(8,128)(2,1)}, bf16[1,3072,128]{2,1,0:T(8,128)(2,1)}, bf16[1,3072,128]{2,1,0:T(8,128)(2,1)}) custom-call(bf16[48,64]{1,0:T(8,128)(2,1)S(1)} %get-tuple-element.9.out_in, bf16[1,3072,128]{2,1,0:T(8,128)(2,1)S(1)} %get-tuple-element.10.gg_in, bf16[1,3072,128]{2,1,0:T(8,128)(2,1)S(1)} %get-tuple-element.11.gu_in), custom_call_target="tpu_custom_call" | custom-call | tf_op jit(solution)/shard_map/finish/pallas_call | solution.py:416

commit v3 on v2

--- a/solution.py
+++ b/solution.py
@@ -30,10 +30,10 @@
 
 
 def kernel(
-    dims, tok, cot, ids, wts, wg_hbm, wu_hbm, wd_hbm, out, gg_hbm, gu_hbm,
-    wgu, wd, wt, picks, sent, got, spread, gath, dx, pair, dxt, pairt, ring_in, ring_out,
+    dims, tok_hbm, cot_hbm, ids_hbm, wts_hbm, wg_hbm, wu_hbm, wd_hbm, out, gg_hbm, gu_hbm,
+    tok, cot, ids, wts, wgu, wd, wt, picks, sent, got, spread, gath, dx, pair, dxt, pairt, ring_in, ring_out,
     tail_in, tail_out,
-    zsum_out, zsum_in, pull, back, home, gbuf, ubuf, lsem, gsend, grecv, zsend, zrecv,
+    zsum_out, zsum_in, pull, back, home, gbuf, ubuf, isem, lsem, gsend, grecv, zsend, zrecv,
     ysend, yrecv, csend, crecv, psend, precv, rsend, rrecv, wsend, wrecv, hsend, hrecv,
 ):
     NG, ZH, NY, feat, toks = dims
@@ -67,6 +67,12 @@
     greet(g, left)
     greet(g, other)
 
+    small = [
+        pltpu.make_async_copy(h, v, isem.at[i])
+        for i, (h, v) in enumerate(((ids_hbm, ids), (wts_hbm, wts), (tok_hbm, tok), (cot_hbm, cot)))
+    ]
+    for copy in small:
+        copy.start()
     loads = [
         pltpu.make_async_copy(wg_hbm.at[0], wgu.at[:, 0:LANES], lsem.at[0]),
         pltpu.make_async_copy(wu_hbm.at[0], wgu.at[:, LANES : 2 * LANES], lsem.at[1]),
@@ -91,6 +97,9 @@
         ).wait_recv()
 
     pending = []
+
+    for copy in small:
+        copy.wait()
 
     who = iota((16, toks), 0)
     first, second = ids[0:1, :] == who, ids[1:2, :] == who
@@ -134,11 +143,10 @@
     block = nn(got[0], spread[0])
     for e in range(1, NG):
         block = block + nn(got[e], spread[e])
-    mine = pl.multiple_of(s * feat, 16)
-    gath[pl.ds(mine, feat), :] = block.astype(BF)
+    gath[z, y, c] = block.astype(BF)
 
     def place(zz, yy, cc):
-        return gath.at[pl.ds(pl.multiple_of(shard_id(zz, yy, cc) * feat, 16), feat), :]
+        return gath.at[zz, yy, cc]
 
     reach = [[NY // 2, NY - 1 - NY // 2] if k % 2 == 0 else [NY - 1 - NY // 2, NY // 2] for k in range(ZH)]
 
@@ -148,9 +156,9 @@
             at = place(wrap(z + k, ZH), wrap(y - step * t, NY), c)
             send(at, at, ysend.at[k, direction, t], yrecv.at[k, direction, t], g, right if direction == 0 else left)
 
-    def across(k, j):
-        at = place(wrap(z + k, ZH), wrap(y + j, NY), c)
-        send(at, at, csend.at[k, j], crecv.at[k, j], g, other)
+    def across(k):
+        at = gath.at[wrap(z + k, ZH), :, c]
+        send(at, at, csend.at[k], crecv.at[k], g, other)
 
     pass_on(0, 0, 0)
     pass_on(0, 1, 0)
@@ -158,39 +166,38 @@
     for k in range(1, ZH):
         to = shard_id(wrap(z + k, ZH), y, c)
         send(at, at, zsend.at[k], zrecv.at[ZH - k], g, to)
-    across(0, 0)
 
     order = [0] + [k for k in (1, ZH - 1) if 0 < k < ZH] + [2]
     order = list(dict.fromkeys(k for k in order if k < ZH))
     lag = {k: 0 if k == 0 else 1 for k in order}
     far = max(max(r) for r in reach)
     def hidden(k, pre, hid):
-        for j in range(NY):
-            arrived(place(wrap(z + k, ZH), wrap(y + j, NY), 1 - c), csend.at[k, j], crecv.at[k, j], g, other)
         q = wrap(z + k, ZH)
-        r = pl.ds(pl.multiple_of(q * rows, 16), rows)
-        return pre + nn(wt[q], gath[r, 0:TOK_LANES]), hid + nn(wd[q], gath[r, 256:ALL_LANES])
+        arrived(gath.at[q, :, 1 - c], csend.at[k], crecv.at[k], g, other)
+        return pre + nn(wt[q], gath[q, :, :, :, 0:TOK_LANES].reshape(rows, TOK_LANES)), hid + nn(
+            wd[q], gath[q, :, :, :, HEAD:ALL_LANES].reshape(rows, ALL_LANES - HEAD)
+        )
 
     pre = jnp.zeros((2 * LANES, TOK_LANES), F32)
     hid = jnp.zeros((LANES, TOK_LANES), F32)
     for wave in range(1, far + 2):
         if wave == far + 1:
             pre, hid = hidden(0, pre, hid)
-        for k in order:
+        for k in order if wave == 1 else order[1:] + order[:1]:
             t = wave - lag[k]
             if t == 0 and k > 0:
                 src = shard_id(wrap(z + k, ZH), y, c)
                 arrived(place(wrap(z + k, ZH), y, c), zsend.at[k], zrecv.at[k], g, src)
                 pass_on(k, 0, 0)
                 pass_on(k, 1, 0)
-                across(k, 0)
-            for direction in (0, 1):
+            for direction in (0, 1) if t >= 0 else ():
                 step = 1 if direction == 0 else -1
                 if 1 <= t <= reach[k][direction]:
                     at = place(wrap(z + k, ZH), wrap(y - step * t, NY), c)
                     arrived(at, ysend.at[k, direction, t - 1], yrecv.at[k, direction, t - 1], g, left if direction == 0 else right)
                     pass_on(k, direction, t)
-                    across(k, (-step * t) % NY)
+            if t == far:
+                across(k)
     for k in order[1:]:
         pre, hid = hidden(k, pre, hid)
     hid = jnp.concatenate([hid[:, 128:384], pltpu.roll(hid[:, 0:128], 96, 1)], axis=1)
@@ -237,7 +244,8 @@
 
     def weight_grads(i):
         r = slice(i * tall, (i + 1) * tall)
-        v = nt(gath[r, 0:TOK_LANES], grads).astype(BF)
+        half = pl.ds((i % 2) * (NY // 2), NY // 2)
+        v = nt(gath[i // 2, half, :, :, 0:TOK_LANES].reshape(tall, TOK_LANES), grads).astype(BF)
         gbuf[r, :] = v[:, 0:LANES]
         ubuf[r, :] = v[:, LANES : 2 * LANES]
 
@@ -371,9 +379,13 @@
             jax.ShapeDtypeStruct(w_gate.shape, BF),
             jax.ShapeDtypeStruct(w_up.shape, BF),
         ),
-        in_specs=[vmem] * 4 + [far_hbm] * 3,
+        in_specs=[far_hbm] * 7,
         out_specs=(vmem, hbm, hbm),
         scratch_shapes=[
+            pltpu.VMEM((feat, toks), BF),
+            pltpu.VMEM((feat, toks), BF),
+            pltpu.VMEM((expert_ids.shape[1], toks), jnp.int32),
+            pltpu.VMEM((route_weight.shape[1], toks), F32),
             pltpu.VMEM((depth, 2 * LANES), BF),
             pltpu.VMEM((ZH, LANES, depth // ZH), BF),
             pltpu.VMEM((ZH, 2 * LANES, depth // ZH), BF),
@@ -381,7 +393,7 @@
             pltpu.VMEM((NG, feat, LANES), BF),
             pltpu.VMEM((NG, feat, LANES), BF),
             pltpu.VMEM((NG, LANES, ALL_LANES), BF),
-            pltpu.VMEM((depth, ALL_LANES), BF),
+            pltpu.VMEM((ZH, NY, 2, feat, ALL_LANES), BF),
             pltpu.VMEM((2,) + half, BF),
             pltpu.VMEM(half, BF),
             pltpu.VMEM((2, NY, feat, LANES), BF),
@@ -397,11 +409,12 @@
             pltpu.VMEM((NG, feat, LANES), BF),
             pltpu.VMEM((depth, LANES), BF),
             pltpu.VMEM((depth, LANES), BF),
+            dma((4,)),
             dma((4 + ZH,)),
             dma((NG,)), dma((NG,)),
             dma((ZH,)), dma((ZH,)),
             dma((ZH, 2, far)), dma((ZH, 2, far)),
-            dma((ZH, NY)), dma((ZH, NY)),
+            dma((ZH,)), dma((ZH,)),
             dma((ZH + 1,)), dma((ZH + 1,)),
             dma((ZH + 1, 2, far)), dma((ZH + 1, 2, far)),
             dma((ZH,)), dma((ZH,)),

time: 76 us -> 74.8 us (0.984)
  Pallas kernels: 75.2 us -> 74 us
    pallas_call x1, Pallas kernels: 74 us -> 72.8 us  [body(): pl.pallas_call(functools.partial(kernel, (NG, ZH, NY, feat, toks)), out_s...]
where the time goes in v3:
time: 74.8 us; the launch traced here: 74.6 us
  Pallas kernels  74 us (99%)
    pallas_call x1, Pallas kernels, body(): pl.pallas_call(functools.partial(kernel, (NG, ZH, NY, feat, toks)), out_s...  72.8 us

profile of v3, /device:TPU:2, one launch (start us, length us, event | category | flops | bytes accessed | tf_op | source)
XLA Modules:
  0.0 74.6 jit_solution(17514393283946672296)
XLA Ops:
  0.6 72.8 %moe_backward.1 = (bf16[48,64]{1,0:T(8,128)(2,1)S(1)}, bf16[1,3072,128]{2,1,0:T(8,128)(2,1)S(1)}, bf16[1,3072,128]{2,1,0:T(8,128)(2,1)S(1)}) custom-call(bf16[48,64]{1,0:T(8,128)(2,1)} %bitcast.5, bf16[48,64]{1,0:T(8,128)(2,1)} %bitcast.6, s32[2,64]{1,0:T(2,128)} %bitcast.7, f32[2,64]{1,0:T(2,128)} %bitcast.8, bf16[1,3072,128]{2,1,0:T(8,128)(2,1)} %wg_hbm.1, ...), custom_call_target="tpu_custom_call" | custom-call | tf_op jit(solution)/shard_map/moe_backward/pallas_call | solution.py:375
  73.5 1.2 %finish.1 = (bf16[48,64]{1,0:T(8,128)(2,1)}, bf16[1,3072,128]{2,1,0:T(8,128)(2,1)}, bf16[1,3072,128]{2,1,0:T(8,128)(2,1)}) custom-call(bf16[48,64]{1,0:T(8,128)(2,1)S(1)} %get-tuple-element.9.out_in, bf16[1,3072,128]{2,1,0:T(8,128)(2,1)S(1)} %get-tuple-element.10.gg_in, bf16[1,3072,128]{2,1,0:T(8,128)(2,1)S(1)} %get-tuple-element.11.gu_in), custom_call_target="tpu_custom_call" | custom-call | tf_op jit(solution)/shard_map/finish/pallas_call | solution.py:429

commit v4 on v3

--- a/solution.py
+++ b/solution.py
@@ -163,7 +163,7 @@
     pass_on(0, 0, 0)
     pass_on(0, 1, 0)
     at = place(z, y, c)
-    for k in range(1, ZH):
+    for k in sorted(range(1, ZH), key=lambda k: -min(k, ZH - k)):
         to = shard_id(wrap(z + k, ZH), y, c)
         send(at, at, zsend.at[k], zrecv.at[ZH - k], g, to)
 

time: 74.8 us -> 74.9 us (level)
  no operation moved by 1% of the time
where the time goes in v4:
time: 74.9 us; the launch traced here: 74.7 us
  Pallas kernels  74.1 us (99%)
    pallas_call x1, Pallas kernels, body(): pl.pallas_call(functools.partial(kernel, (NG, ZH, NY, feat, toks)), out_s...  72.9 us

profile of v4, /device:TPU:2, one launch (start us, length us, event | category | flops | bytes accessed | tf_op | source)
XLA Modules:
  0.0 74.7 jit_solution(17788602496080270644)
XLA Ops:
  0.6 72.9 %moe_backward.1 = (bf16[48,64]{1,0:T(8,128)(2,1)S(1)}, bf16[1,3072,128]{2,1,0:T(8,128)(2,1)S(1)}, bf16[1,3072,128]{2,1,0:T(8,128)(2,1)S(1)}) custom-call(bf16[48,64]{1,0:T(8,128)(2,1)} %bitcast.5, bf16[48,64]{1,0:T(8,128)(2,1)} %bitcast.6, s32[2,64]{1,0:T(2,128)} %bitcast.7, f32[2,64]{1,0:T(2,128)} %bitcast.8, bf16[1,3072,128]{2,1,0:T(8,128)(2,1)} %wg_hbm.1, ...), custom_call_target="tpu_custom_call" | custom-call | tf_op jit(solution)/shard_map/moe_backward/pallas_call | solution.py:375
  73.6 1.2 %finish.1 = (bf16[48,64]{1,0:T(8,128)(2,1)}, bf16[1,3072,128]{2,1,0:T(8,128)(2,1)}, bf16[1,3072,128]{2,1,0:T(8,128)(2,1)}) custom-call(bf16[48,64]{1,0:T(8,128)(2,1)S(1)} %get-tuple-element.9.out_in, bf16[1,3072,128]{2,1,0:T(8,128)(2,1)S(1)} %get-tuple-element.10.gg_in, bf16[1,3072,128]{2,1,0:T(8,128)(2,1)S(1)} %get-tuple-element.11.gu_in), custom_call_target="tpu_custom_call" | custom-call | tf_op jit(solution)/shard_map/finish/pallas_call | solution.py:429
